TPU v7x, 128 devices: a whole 4x4x4 slice. The times are simulated.
128 devices in a mesh: layer: 4 (over x_hi, core), feat: 16 (over z, y), par: 2 (over x_lo).
Axes of the slice: x: 4 (x_hi: 2, x_lo: 2; x = x_hi * 2 + x_lo), y: 4, z: 4, core: 2. Of those that a mesh axis runs over, the one named last changes fastest.
Arguments:
- residual: bfloat16 [4, 512, 2304], P('layer'), may hold values from -6 to 6
- norm_gain: float32 [4, 2304], P('layer'), may hold values from 0.5 to 1.5
- gate_weight: bfloat16 [4, 2304, 9216], P('layer', None, ('feat', 'par')), may hold values from -0.125 to 0.125
- up_weight: bfloat16 [4, 2304, 9216], P('layer', None, ('feat', 'par')), may hold values from -0.125 to 0.125
- down_weight: bfloat16 [4, 9216, 2304], P('layer', ('feat', 'par')), may hold values from -0.0625 to 0.0625
- enc_weight: float32 [4, 2304, 8192], P('layer', 'par', 'feat'), may hold values from -0.125 to 0.125
- enc_bias: float32 [4, 8192], P('layer', 'feat'), may hold values from -1 to 0.5
- dec_weight: bfloat16 [4, 2, 2, 8192, 2304], P('layer', 'par', None, 'feat'), may hold values from -0.0625 to 0.0625
- dec_bias: float32 [4, 2304], replicated, may hold values from -3 to 3
Outputs:
- enc_grad: float32 [4, 2304, 8192], P('layer', 'par', 'feat')
- enc_bias_grad: float32 [4, 8192], P('layer', 'feat')
- dec_grad: bfloat16 [4, 2, 2, 8192, 2304], P('layer', 'par', None, 'feat')
All inputs are finite; a program needn't handle non-finite values.
Results may differ from a plain program's by a relative error of at most 0.007.
Values may be sent and summed in bfloat16 or wider, within the bound.
A program may use at most 192 MiB of HBM per device.

v0:
```python
import jax
import jax.numpy as jnp
from jax import lax
from jax.sharding import PartitionSpec as P


def rms_normed(rows_in, gain_row):
    values = rows_in.astype(jnp.float32)
    scaling = lax.rsqrt(jnp.mean(values * values, axis=-1, keepdims=True) + 1e-06)
    return (values * scaling * gain_row).astype(jnp.bfloat16)


def shards(
    residual,
    norm_gain,
    gate_weight,
    up_weight,
    down_weight,
    enc_weight,
    enc_bias,
    dec_weight,
    dec_bias,
):
    highest = lax.Precision.HIGHEST
    source = lax.axis_index("layer")
    parity = lax.axis_index("par")
    slot_count = dec_weight.shape[2]
    normed = rms_normed(residual[0], norm_gain[0])
    tokens, model_width = normed.shape
    gate_value = jnp.dot(normed, gate_weight[0], preferred_element_type=jnp.float32)
    up_value = jnp.dot(normed, up_weight[0], preferred_element_type=jnp.float32)
    hidden = (jax.nn.gelu(gate_value, approximate=True) * up_value).astype(jnp.bfloat16)
    target_part = jnp.dot(hidden, down_weight[0], preferred_element_type=jnp.float32)
    half_width = enc_weight.shape[1]
    my_rows = lax.dynamic_slice_in_dim(normed, parity * half_width, half_width, 1).astype(
        jnp.float32
    )
    pre_part = jnp.dot(my_rows, enc_weight[0], precision=highest)
    pre_act = lax.psum(pre_part, "par") + enc_bias[0]
    positive = jnp.maximum(pre_act, 0.0)
    actives = (positive * positive).astype(jnp.bfloat16)
    slot_ids = jnp.arange(slot_count, dtype=jnp.int32)
    slot_live = 2 * slot_ids + parity >= source
    live_float = slot_live.astype(jnp.float32)
    decoders = dec_weight[0, 0]
    recon_parts = (
        jnp.einsum("tf,jfd->jtd", actives, decoders, preferred_element_type=jnp.float32)
        * live_float[:, None, None]
    )
    bias_slots = lax.dynamic_index_in_dim(
        dec_bias.reshape(slot_count, 2, model_width), parity, 1, keepdims=False
    )
    full_target = lax.psum(target_part, ("feat", "par"))
    all_targets = lax.all_gather(full_target[None], "layer", axis=0, tiled=True)
    target_slots = lax.dynamic_index_in_dim(
        all_targets.reshape(slot_count, 2, tokens, model_width), parity, 1, keepdims=False
    )
    summed_rows = lax.psum(recon_parts, ("layer", "feat"))
    err_full = summed_rows + bias_slots[:, None, :]
    err_full = err_full - target_slots
    errors = (err_full * 0.0625).astype(jnp.bfloat16)
    masked = errors * slot_live.astype(jnp.bfloat16)[:, None, None]
    back_part = jnp.einsum("jtd,jfd->tf", masked, decoders, preferred_element_type=jnp.float32)
    back_grad = lax.psum(back_part.astype(jnp.bfloat16), "par").astype(jnp.float32)
    d_pre = back_grad * 2.0 * positive
    enc_grad = lax.dot_general(my_rows, d_pre, (((0,), (0,)), ((), ())), precision=highest)
    bias_grad = jnp.sum(d_pre, axis=0)
    dec_grad = jnp.einsum(
        "tf,jtd->jfd", actives, masked, preferred_element_type=jnp.float32
    ).astype(jnp.bfloat16)
    return (enc_grad[None], bias_grad[None], dec_grad[None, None])


def solution(mesh):
    return jax.shard_map(
        shards,
        mesh=mesh,
        in_specs=(
            P("layer", None, None),
            P("layer", None),
            P("layer", None, ("feat", "par")),
            P("layer", None, ("feat", "par")),
            P("layer", ("feat", "par"), None),
            P("layer", "par", "feat"),
            P("layer", "feat"),
            P("layer", "par", None, "feat", None),
            P(),
        ),
        out_specs=(
            P("layer", "par", "feat"),
            P("layer", "feat"),
            P("layer", "par", None, "feat", None),
        ),
        check_vma=False,
    )
```

profile of v0, /device:TPU:1, one launch (start us, length us, event | category | flops | bytes accessed | tf_op | source)
XLA Modules:
  0.0 1276.6 jit_solution(10719600831375024537)
XLA Ops:
  7.2 0.0 copy-start
  7.2 0.0 all-reduce.5.cloned.1.call-start
  7.2 0.0 copy-start.6
  7.2 2.4 multiply_reduce_fusion
  9.6 4.2 convert_bitcast_fusion
  13.8 0.0 copy-done.6
  13.8 0.1 dynamic-slice
  13.9 0.0 copy-done
  13.9 4.9 fusion.12
  18.8 0.0 all-reduce.5.cloned.1.call-update
  18.9 0.0 copy-start.2
  18.9 0.0 all-reduce.9.cloned.1.call-start
  18.9 3.2 fusion.43
  22.2 0.0 copy-done.2
  22.2 6.3 convolution_bitcast_fusion
  28.4 0.0 copy-start.5
  28.4 0.0 all-reduce.9.cloned.1.call-update
  28.5 0.0 all-reduce.7.cloned.1.call-start
  28.5 40.3 %all-reduce.5.cloned.1.call-done = f32[512,512]{1,0:T(8,128)} async-done(((f32[512,512]{1,0:T(8,128)}), f32[512,512]{1,0:T(8,128)}) %all-reduce.5.cloned.1.call-update) | async-done | bytes 1048592 | tf_op jit(solution)/shard_map/psum | solution.py:39
  68.8 0.0 copy-done.5
  68.8 8.9 multiply_bitcast_fusion
  77.8 0.0 all-reduce.7.cloned.1.call-update
  77.8 0.0 copy-start.4
  77.8 0.0 all-gather.2.cloned.1.call-start
  77.8 314.6 %all-reduce.9.cloned.1.call-done = f32[1,512,2304]{2,1,0:T(8,128)} async-done(((f32[1,512,2304]{2,1,0:T(8,128)}), f32[1,512,2304]{2,1,0:T(8,128)}) %all-reduce.9.cloned.1.call-update) | async-done | bytes 4718608 | tf_op jit(solution)/shard_map/psum | solution.py:53
  392.4 0.0 all-gather.2.cloned.1.call-update
  392.5 0.2 all-reduce.11.cloned.1.call-start
  392.7 0.0 copy-done.4
  392.8 668.2 %all-reduce.7.cloned.1.call-done = f32[2,512,2304]{2,1,0:T(8,128)} async-done(((f32[2,512,2304]{2,1,0:T(8,128)}), f32[2,512,2304]{2,1,0:T(8,128)}) %all-reduce.7.cloned.1.call-update) | async-done | bytes 9437200 | tf_op jit(solution)/shard_map/psum | solution.py:58
  1061.0 149.9 %all-gather.2.cloned.1.call-done = f32[4,512,2304]{2,1,0:T(8,128)} async-done(((f32[1,512,2304]{2,1,0:T(8,128)}), f32[4,512,2304]{2,1,0:T(8,128)}) %all-gather.2.cloned.1.call-update) | async-done | bytes 18874384 | tf_op jit(solution)/shard_map/all_gather | solution.py:54
  1210.8 10.1 fusion.5
  1220.9 0.0 copy-start.3
  1220.9 7.3 fusion.22
  1228.2 0.0 all-reduce.11.cloned.1.call-update
  1228.2 0.0 copy-done.3
  1228.2 6.7 fusion.2
  1234.9 0.0 copy-start.1
  1234.9 6.8 copy.17
  1241.7 21.0 %all-reduce.11.cloned.1.call-done = bf16[512,512]{1,0:T(8,128)(2,1)} async-done(((bf16[512,512]{1,0:T(8,128)(2,1)}), bf16[512,512]{1,0:T(8,128)(2,1)}) %all-reduce.11.cloned.1.call-update) | async-done | bytes 524304 | tf_op jit(solution)/shard_map/psum | solution.py:64
  1262.7 1.8 fusion.48
  1264.6 5.5 convolution_bitcast_fusion.1
  1270.1 0.0 copy-done.1
  (7 shorter events, 0.1 us)
Async XLA Ops:
  7.2 6.7 copy-start
  7.2 61.7 %all-reduce.5.cloned.1.call-start = ((), (), s32[]{:S(2)}) async-start(), calls=%async_computation | async-start | bytes 2097152 | tf_op jit(solution)/shard_map/psum | solution.py:39
  7.2 6.5 copy-start.6
  18.9 3.3 copy-start.2
  18.9 373.6 %all-reduce.9.cloned.1.call-start = ((), (), s32[]{:S(2)}) async-start(), calls=%async_computation.2 | async-start | bytes 9437184 | tf_op jit(solution)/shard_map/psum | solution.py:53
  28.4 40.4 %copy-start.5 = (f32[1,512]{1,0:T(1,128)S(1)}, f32[1,512]{1,0:T(1,128)}, u32[]{:S(2)}) copy-start(f32[1,512]{1,0:T(1,128)} %param.15) | copy-start | bytes 6148
  28.5 1032.5 %all-reduce.7.cloned.1.call-start = ((), (), s32[]{:S(2)}) async-start(), calls=%async_computation.1 | async-start | bytes 18874368 | tf_op jit(solution)/shard_map/psum | solution.py:58
  77.8 314.9 %copy-start.4 = (f32[4,2304]{1,0:T(4,128)S(1)}, f32[4,2304]{1,0:T(4,128)}, u32[]{:S(2)}) copy-start(f32[4,2304]{1,0:T(4,128)} %param.17) | copy-start | bytes 110596
  77.8 1133.0 %all-gather.2.cloned.1.call-start = ((), (), s32[]{:S(2)}) async-start(), calls=%async_computation.3 | async-start | bytes 23592960 | tf_op jit(solution)/shard_map/all_gather | solution.py:54
  392.5 870.3 %all-reduce.11.cloned.1.call-start = ((), (), s32[]{:S(2)}) async-start(), calls=%async_computation.4 | async-start | bytes 1048576 | tf_op jit(solution)/shard_map/psum | solution.py:64
  1220.9 7.3 copy-start.3
  1234.9 35.2 %copy-start.1 = (f32[1,1152,512]{2,1,0:T(8,128)S(1)}, f32[1,1152,512]{2,1,0:T(8,128)}, u32[]{:S(2)}) copy-start(f32[1,1152,512]{2,1,0:T(8,128)} %param.14) | copy-start | bytes 7077892
Sparse Core Ops, SparseCore 0:
  19.0 49.8 all-reduce.4
  72.1 320.3 all-reduce.8
  395.1 665.8 all-reduce.6
  1062.6 148.1 all-gather.1
  1228.3 34.3 all-reduce.10
where the time goes:
time: 1280 us
  waiting for transfers between devices  1190 us (93%)
  matrix products  42.9 us (3%)
  other arithmetic  18.5 us (1%)
  between operations  13.9 us (1%)
    psum x1, waiting for transfers between devices, shards(): summed_rows = lax.psum(recon_parts, ('layer', 'feat'))  668 us
    psum x1, waiting for transfers between devices, shards(): full_target = lax.psum(target_part, ('feat', 'par'))  315 us
    all_gather x1, waiting for transfers between devices, shards(): all_targets = lax.all_gather(full_target[None], 'layer', axis=0, tiled=True)  150 us
    psum x1, waiting for transfers between devices, shards(): pre_act = lax.psum(pre_part, 'par') + enc_bias[0]  40.3 us
  transfers between devices with their start and end apart: 5, of which 5 were waited for; matrix products, arithmetic and copies ran while one was open for 3% of the time, Pallas kernels for 0%

commit v1 on v0

--- a/solution.py
+++ b/solution.py
@@ -50,7 +50,7 @@
     bias_slots = lax.dynamic_index_in_dim(
         dec_bias.reshape(slot_count, 2, model_width), parity, 1, keepdims=False
     )
-    full_target = lax.psum(target_part, ("feat", "par"))
+    full_target = jnp.sum(lax.all_gather(target_part, ("feat", "par")), axis=0)
     all_targets = lax.all_gather(full_target[None], "layer", axis=0, tiled=True)
     target_slots = lax.dynamic_index_in_dim(
         all_targets.reshape(slot_count, 2, tokens, model_width), parity, 1, keepdims=False

time: 1280 us -> 3900 us (3.05)
  waiting for transfers between devices: 1190 us -> 3760 us
  other arithmetic: 18.5 us -> 65.3 us
    all_gather x0 -> x1, waiting for transfers between devices: none -> 3040 us  [shards(): full_target = jnp.sum(lax.all_gather(target_part, ('feat', 'par')), axis=0)]
    psum x1 -> x0, waiting for transfers between devices: 315 us -> none  [shards(): full_target = lax.psum(target_part, ('feat', 'par'))]
    all_gather x1, waiting for transfers between devices: 150 us -> 0.01 us  [shards(): all_targets = lax.all_gather(full_target[None], 'layer', axis=0, tiled=True)]
    psum x1, waiting for transfers between devices: 668 us -> 542 us  [shards(): summed_rows = lax.psum(recon_parts, ('layer', 'feat'))]
    psum x1, waiting for transfers between devices: 40.3 us -> 141 us  [shards(): pre_act = lax.psum(pre_part, 'par') + enc_bias[0]]
    reduce_sum x0 -> x1, other arithmetic: none -> 47.9 us  [shards(): full_target = jnp.sum(lax.all_gather(target_part, ('feat', 'par')), axis=0)]
  transfers between devices with their start and end apart: 5 -> 5, of which waited for: 5 -> 4; matrix products, arithmetic and copies ran while one was open for 3% -> 2% of each run, Pallas kernels for 0% -> 0%
where the time goes in v1:
time: 3900 us
  waiting for transfers between devices  3760 us (96%)
  other arithmetic  65.3 us (2%)
  matrix products  43 us (1%)
    all_gather x1, waiting for transfers between devices, shards(): full_target = jnp.sum(lax.all_gather(target_part, ('feat', 'par')), axis=0)  3040 us
    psum x1, waiting for transfers between devices, shards(): summed_rows = lax.psum(recon_parts, ('layer', 'feat'))  542 us
    psum x1, waiting for transfers between devices, shards(): pre_act = lax.psum(pre_part, 'par') + enc_bias[0]  141 us
  transfers between devices with their start and end apart: 5, of which 4 were waited for; matrix products, arithmetic and copies ran while one was open for 2% of the time, Pallas kernels for 0%

profile of v1, /device:TPU:1, one launch (start us, length us, event | category | flops | bytes accessed | tf_op | source)
XLA Modules:
  0.0 3895.8 jit_solution(4474386518046987420)
XLA Ops:
  8.0 0.0 copy-start
  8.0 0.0 all-reduce.4.cloned.1.call-start
  8.1 0.0 copy-start.7
  8.1 2.4 multiply_reduce_fusion
  10.4 4.1 convert_bitcast_fusion
  14.6 0.0 copy-done.7
  14.6 0.1 dynamic-slice
  14.7 0.0 copy-done
  14.7 4.9 fusion.12
  19.6 0.0 all-reduce.4.cloned.1.call-update
  19.7 0.0 copy-start.2
  19.7 0.0 all-gather.5.cloned.1.call-start
  19.7 3.2 fusion.43
  23.0 0.0 copy-done.2
  23.0 6.3 fusion.17
  29.2 0.0 copy-start.6
  29.3 0.0 all-gather.5.cloned.1.call-update
  29.3 0.0 all-reduce.6.cloned.1.call-start
  29.3 140.6 %all-reduce.4.cloned.1.call-done = f32[512,512]{1,0:T(8,128)} async-done(((f32[512,512]{1,0:T(8,128)}), f32[512,512]{1,0:T(8,128)}) %all-reduce.4.cloned.1.call-update) | async-done | bytes 1048592 | tf_op jit(solution)/shard_map/psum | solution.py:39
  170.0 0.0 copy-done.6
  170.0 8.9 multiply_bitcast_fusion
  178.9 0.0 all-reduce.6.cloned.1.call-update
  178.9 0.0 all-gather.7.cloned.1.call-start
  179.0 3036.1 %all-gather.5.cloned.1.call-done = f32[16384,2304]{1,0:T(8,128)} async-done(((f32[512,2304]{1,0:T(8,128)}), f32[16384,2304]{1,0:T(8,128)}) %all-gather.5.cloned.1.call-update) | async-done | bytes 150994960 | tf_op jit(solution)/shard_map/all_gather | solution.py:53
  3215.1 47.9 %reduce_sum.28 = f32[512,2304]{1,0:T(8,128)} reduce(f32[32,512,2304]{2,1,0:T(8,128)} %bitcast.10, f32[]{:T(128)} %constant.16.clone.1), dimensions={0}, to_apply=%region_3.4 | reduce | flops 36569088 | bytes 155713536 | tf_op jit(solution)/shard_map/reduce_sum | solution.py:53
  3263.0 0.0 copy-start.5
  3263.0 0.0 all-gather.7.cloned.1.call-update
  3263.0 0.2 all-reduce.8.cloned.1.call-start
  3263.3 0.5 copy-done.5
  3263.9 542.1 %all-reduce.6.cloned.1.call-done = f32[2,512,2304]{2,1,0:T(8,128)} async-done(((f32[2,512,2304]{2,1,0:T(8,128)}), f32[2,512,2304]{2,1,0:T(8,128)}) %all-reduce.6.cloned.1.call-update) | async-done | bytes 9437200 | tf_op jit(solution)/shard_map/psum | solution.py:58
  3806.0 0.0 all-gather.7.cloned.1.call-done
  3806.0 10.1 fusion.5
  3816.1 0.0 copy-start.3
  3816.1 7.3 fusion.23
  3823.3 0.0 all-reduce.8.cloned.1.call-update
  3823.3 0.0 copy-done.3
  3823.4 6.8 fusion.2
  3830.1 0.0 copy-start.1
  3830.1 6.8 copy.15
  3836.9 45.4 %all-reduce.8.cloned.1.call-done = bf16[512,512]{1,0:T(8,128)(2,1)} async-done(((bf16[512,512]{1,0:T(8,128)(2,1)}), bf16[512,512]{1,0:T(8,128)(2,1)}) %all-reduce.8.cloned.1.call-update) | async-done | bytes 524304 | tf_op jit(solution)/shard_map/psum | solution.py:64
  3882.2 0.0 copy-start.4
  3882.2 5.6 convolution_bitcast_fusion
  3887.8 0.0 copy-done.4
  3887.8 0.8 fusion.48
  3888.6 0.0 copy-done.1
  (7 shorter events, 0.1 us)
Async XLA Ops:
  8.0 6.7 copy-start
  8.0 162.0 %all-reduce.4.cloned.1.call-start = ((), (), s32[]{:S(2)}) async-start(), calls=%async_computation | async-start | bytes 2097152 | tf_op jit(solution)/shard_map/psum | solution.py:39
  8.1 6.5 copy-start.7
  19.7 3.3 copy-start.2
  19.7 3195.4 %all-gather.5.cloned.1.call-start = ((), (), s32[]{:S(2)}) async-start(), calls=%async_computation.3 | async-start | bytes 155713536 | tf_op jit(solution)/shard_map/all_gather | solution.py:53
  29.2 140.7 %copy-start.6 = (f32[1,512]{1,0:T(1,128)S(1)}, f32[1,512]{1,0:T(1,128)}, u32[]{:S(2)}) copy-start(f32[1,512]{1,0:T(1,128)} %param.15) | copy-start | bytes 6148
  29.3 3776.7 %all-reduce.6.cloned.1.call-start = ((), (), s32[]{:S(2)}) async-start(), calls=%async_computation.1 | async-start | bytes 18874368 | tf_op jit(solution)/shard_map/psum | solution.py:58
  178.9 3627.1 %all-gather.7.cloned.1.call-start = ((), (), s32[]{:S(2)}) async-start(), calls=%async_computation.4 | async-start | bytes 23592960 | tf_op jit(solution)/shard_map/all_gather | solution.py:54
  3263.0 0.8 copy-start.5
  3263.0 619.2 %all-reduce.8.cloned.1.call-start = ((), (), s32[]{:S(2)}) async-start(), calls=%async_computation.2 | async-start | bytes 1048576 | tf_op jit(solution)/shard_map/psum | solution.py:64
  3816.1 7.3 copy-start.3
  3830.1 58.5 %copy-start.1 = (f32[1,1152,512]{2,1,0:T(8,128)S(1)}, f32[1,1152,512]{2,1,0:T(8,128)}, u32[]{:S(2)}) copy-start(f32[1,1152,512]{2,1,0:T(8,128)} %param.14) | copy-start | bytes 7077892
  3882.2 5.6 copy-start.4
Sparse Core Ops, SparseCore 0:
  19.8 150.1 all-reduce.3
  179.0 3626.8 all-reduce.5
  3823.5 58.7 all-reduce.7
Sparse Core Ops, SparseCore 1:
  29.4 3185.7 all-gather.4
  3263.1 134.2 all-gather.6

commit v2 on v0

--- a/solution.py
+++ b/solution.py
@@ -50,7 +50,7 @@
     bias_slots = lax.dynamic_index_in_dim(
         dec_bias.reshape(slot_count, 2, model_width), parity, 1, keepdims=False
     )
-    full_target = lax.psum(target_part, ("feat", "par"))
+    full_target = lax.psum(lax.psum(target_part, "feat"), "par")
     all_targets = lax.all_gather(full_target[None], "layer", axis=0, tiled=True)
     target_slots = lax.dynamic_index_in_dim(
         all_targets.reshape(slot_count, 2, tokens, model_width), parity, 1, keepdims=False

time: 1280 us -> 1160 us (0.906)
  waiting for transfers between devices: 1190 us -> 1070 us
    psum x2, waiting for transfers between devices: 355 us -> 256 us  [shards(): full_target = lax.psum(lax.psum(target_part, 'feat'), 'par')]
    psum x1, waiting for transfers between devices: 668 us -> 646 us  [shards(): summed_rows = lax.psum(recon_parts, ('layer', 'feat'))]
  transfers between devices with their start and end apart: 5 -> 5, of which waited for: 5 -> 5; matrix products, arithmetic and copies ran while one was open for 3% -> 2% of each run, Pallas kernels for 0% -> 0%
where the time goes in v2:
time: 1160 us
  waiting for transfers between devices  1070 us (92%)
  matrix products  41.9 us (4%)
  other arithmetic  17 us (1%)
  between operations  13.9 us (1%)
    psum x1, waiting for transfers between devices, shards(): summed_rows = lax.psum(recon_parts, ('layer', 'feat'))  646 us
    psum x2, waiting for transfers between devices, shards(): full_target = lax.psum(lax.psum(target_part, 'feat'), 'par')  256 us
    all_gather x1, waiting for transfers between devices, shards(): all_targets = lax.all_gather(full_target[None], 'layer', axis=0, tiled=True)  150 us
  transfers between devices with their start and end apart: 5, of which 5 were waited for; matrix products, arithmetic and copies ran while one was open for 2% of the time, Pallas kernels for 0%

profile of v2, /device:TPU:1, one launch (start us, length us, event | category | flops | bytes accessed | tf_op | source)
XLA Modules:
  0.0 1155.6 jit_solution(15705061451066129697)
XLA Ops:
  7.2 0.0 copy-start
  7.2 0.0 all-reduce.8.cloned.1.call-start
  7.2 2.4 multiply_reduce_fusion
  9.6 0.7 reduce
  10.3 3.1 fusion.43
  13.4 7.0 fusion.17
  20.4 0.0 all-reduce.8.cloned.1.call-update
  20.4 0.0 all-reduce.12.cloned.1.call-start
  20.5 0.1 dynamic-slice
  20.6 2.0 convert_bitcast_fusion
  22.6 0.0 copy-start.2
  22.6 2.1 copy-done.2
  24.7 0.0 copy-done
  24.7 0.0 copy-start.5
  24.7 3.3 fusion.12
  28.1 104.1 %all-reduce.8.cloned.1.call-done = f32[512,2304]{1,0:T(8,128)} async-done(((f32[512,2304]{1,0:T(8,128)}), f32[512,2304]{1,0:T(8,128)}) %all-reduce.8.cloned.1.call-update) | async-done | bytes 4718608 | tf_op jit(solution)/shard_map/psum | solution.py:53
  132.1 0.0 all-reduce.12.cloned.1.call-update
  132.1 0.0 all-reduce.6.cloned.1.call-start
  132.2 151.8 %all-reduce.12.cloned.1.call-done = (f32[1,512,2304]{2,1,0:T(8,128)}, f32[512,512]{1,0:T(8,128)}) async-done(((f32[1,512,2304]{2,1,0:T(8,128)}, f32[512,512]{1,0:T(8,128)}), (f32[1,512,2304]{2,1,0:T(8,128)}, f32[512,512]{1,0:T(8,128)})) %all-reduce.12.cloned.1.call-update) | async-done | bytes 5767184 | tf_op jit(solution)/shard_map/psum | solution.py:53
  284.0 0.0 copy-done.5
  284.0 8.9 multiply_bitcast_fusion
  293.0 0.0 all-reduce.6.cloned.1.call-update
  293.0 0.0 copy-start.4
  293.0 0.0 all-gather.2.cloned.1.call-start
  293.0 0.5 all-gather.2.cloned.1.call-update
  293.6 0.2 all-reduce.10.cloned.1.call-start
  293.8 0.0 copy-done.4
  293.9 646.4 %all-reduce.6.cloned.1.call-done = f32[2,512,2304]{2,1,0:T(8,128)} async-done(((f32[2,512,2304]{2,1,0:T(8,128)}), f32[2,512,2304]{2,1,0:T(8,128)}) %all-reduce.6.cloned.1.call-update) | async-done | bytes 9437200 | tf_op jit(solution)/shard_map/psum | solution.py:58
  940.3 149.5 %all-gather.2.cloned.1.call-done = f32[4,512,2304]{2,1,0:T(8,128)} async-done(((f32[1,512,2304]{2,1,0:T(8,128)}), f32[4,512,2304]{2,1,0:T(8,128)}) %all-gather.2.cloned.1.call-update) | async-done | bytes 18874384 | tf_op jit(solution)/shard_map/all_gather | solution.py:54
  1089.8 10.1 fusion.5
  1099.9 0.0 copy-start.3
  1099.9 7.3 fusion.23
  1107.2 0.0 all-reduce.10.cloned.1.call-update
  1107.2 0.0 copy-done.3
  1107.2 6.7 fusion.2
  1113.9 0.0 copy-start.1
  1113.9 6.8 copy.17
  1120.7 21.0 %all-reduce.10.cloned.1.call-done = bf16[512,512]{1,0:T(8,128)(2,1)} async-done(((bf16[512,512]{1,0:T(8,128)(2,1)}), bf16[512,512]{1,0:T(8,128)(2,1)}) %all-reduce.10.cloned.1.call-update) | async-done | bytes 524304 | tf_op jit(solution)/shard_map/psum | solution.py:64
  1141.7 1.8 fusion.48
  1143.6 5.5 convolution_bitcast_fusion
  1149.1 0.0 copy-done.1
  (6 shorter events, 0.1 us)
Async XLA Ops:
  7.2 17.6 %copy-start = (f32[1,1152,512]{2,1,0:T(8,128)S(1)}, f32[1,1152,512]{2,1,0:T(8,128)}, u32[]{:S(2)}) copy-start(f32[1,1152,512]{2,1,0:T(8,128)} %param.14) | copy-start | bytes 7077892
  7.2 124.9 %all-reduce.8.cloned.1.call-start = ((), (), s32[]{:S(2)}) async-start(), calls=%async_computation.1 | async-start | bytes 9437184 | tf_op jit(solution)/shard_map/psum | solution.py:53
  20.4 263.6 %all-reduce.12.cloned.1.call-start = ((), (), s32[]{:S(2)}) async-start(), calls=%async_computation.4 | async-start | bytes 11534336 | tf_op jit(solution)/shard_map/psum | solution.py:53
  22.6 2.2 copy-start.2
  24.7 259.3 %copy-start.5 = (f32[1,512]{1,0:T(1,128)S(1)}, f32[1,512]{1,0:T(1,128)}, u32[]{:S(2)}) copy-start(f32[1,512]{1,0:T(1,128)} %param.15) | copy-start | bytes 6148
  132.1 808.2 %all-reduce.6.cloned.1.call-start = ((), (), s32[]{:S(2)}) async-start(), calls=%async_computation | async-start | bytes 18874368 | tf_op jit(solution)/shard_map/psum | solution.py:58
  293.0 0.8 copy-start.4
  293.0 796.8 %all-gather.2.cloned.1.call-start = ((), (), s32[]{:S(2)}) async-start(), calls=%async_computation.2 | async-start | bytes 23592960 | tf_op jit(solution)/shard_map/all_gather | solution.py:54
  293.6 848.1 %all-reduce.10.cloned.1.call-start = ((), (), s32[]{:S(2)}) async-start(), calls=%async_computation.3 | async-start | bytes 1048576 | tf_op jit(solution)/shard_map/psum | solution.py:64
  1099.9 7.3 copy-start.3
  1113.9 35.2 %copy-start.1 = (f32[1,1152,512]{2,1,0:T(8,128)S(1)}, f32[1,1152,512]{2,1,0:T(8,128)}, u32[]{:S(2)}) copy-start(f32[1,1152,512]{2,1,0:T(8,128)} %param.14) | copy-start | bytes 7077892
Sparse Core Ops, SparseCore 0:
  20.6 111.5 all-reduce.7
  135.5 148.4 all-reduce.11
  293.1 647.1 all-reduce.5
  941.8 147.9 all-gather.1
  1107.3 34.3 all-reduce.9
